TPU v7x, 256 devices: a whole 4x4x8 slice. The times are simulated.
256 devices in a mesh: rows: 64 (over y, z, core), feat: 4 (over x).
Axes of the slice: x: 4, y: 4, z: 8, core: 2. Of those that a mesh axis runs over, the one named last changes fastest.
Arguments:
- gradients: bfloat16 [32768, 128], P('rows'), may hold values from -6 to 6
- hessians: bfloat16 [32768], P('rows'), may hold values from 0.25 to 2
- bin_words: int32 [128, 32768], P('feat', 'rows'), may hold values from 0 to 4095, as said below
- children: int32 [3, 32768], P(None, 'rows'), may hold values from 0 to 1, as said below
- split_feature: int32 [14], replicated, may hold values from 0 to 255
- split_bin: int32 [14], replicated, may hold values from 0 to 62
Outputs:
- split_gain_one: float32 [128, 256], P('rows', 'feat')
- split_gain_two: float32 [256, 256], P('rows', 'feat')
- split_gain_three: float32 [512, 256], P('rows', 'feat')
- child_scores: float32 [3, 64, 2, 128], P(None, 'rows')
Inputs may be any that keep to these rules, and one draw needn't show every extreme that they name: `children`: of the 512 rows of one device, at most 3 / 4, 1 / 2 and 1 / 4 of 512 lie in one node at depths 1, 2 and 3; every device reaches each of these bounds in some node. `bin_words`: word w of panel p, six bits a feature with the lowest bits first, holds the bins of the panel's features 2 w and 2 w + 1, numbered within the panel of 64 features; slots past the panel's last feature are zero. Every bin is below 64.
All inputs are finite; a program needn't handle non-finite values.
Results may differ from a plain program's by a relative error of at most 0.0003.
Values may be sent and summed in bfloat16 or wider, within the bound.
A program may use at most 64 MiB of HBM per device.

v0:
```python
import jax
import jax.numpy as jnp
from jax import lax
from jax.sharding import PartitionSpec as P

FEATURES = 256
BINS = 64
OUT = 128
LEVELS = 3
penalty = 1.0


def as_sent(array):
    return jax.tree.map(lambda a: a.astype(jnp.bfloat16) if a.dtype == jnp.float32 else a, array)


def swapped(block, axis, stride):
    count = lax.axis_size(axis)
    route = []
    for low in range(count):
        high = low | 1 << stride
        if high != low and high < count:
            route += [(low, high), (high, low)]
    return lax.ppermute(block, axis, route)


def unpack_codes(packed):
    shifts = 6 * jnp.arange(2, dtype=jnp.int32)
    pieces = jnp.bitwise_and(jnp.right_shift(packed[:, None, :], shifts[None, :, None]), 63)
    return pieces.reshape(-1, packed.shape[-1])


def split_terms(cumulative, hess_cum):
    total_sum = cumulative[..., -1:, :]
    hess_total = hess_cum[..., -1:]
    right_sum = total_sum - cumulative
    hess_right = hess_total - hess_cum
    split_score = (
        jnp.sum(cumulative * cumulative, -1) / (hess_cum + penalty)
        + jnp.sum(right_sum * right_sum, -1) / (hess_right + penalty)
        - jnp.sum(total_sum * total_sum, -1) / (hess_total + penalty)
    ) / OUT
    return (split_score, right_sum, hess_right)


def front_index(marked, slot_total):
    running = jnp.cumsum(marked.astype(jnp.int32))
    wanted = jnp.arange(slot_total, dtype=jnp.int32) + 1
    source = jnp.searchsorted(running, wanted, side="left")
    filled = wanted <= running[-1]
    return (jnp.minimum(source, marked.shape[0] - 1), filled)


def pick_rows(values, source, filled):
    taken = jnp.take(values, source, axis=0)
    return jnp.where(filled[:, None], taken, jnp.zeros_like(taken))


def pick_slots(values, source, filled):
    taken = jnp.take(values, source, axis=0)
    return jnp.where(filled, taken, jnp.zeros_like(taken))


def pick_columns(values, source, filled):
    taken = jnp.take(values, source, axis=1)
    return jnp.where(filled[None, :], taken, jnp.zeros_like(taken))


def build_hist(bin_codes, grad_rows, hess_rows, block_rows):
    feat_count = bin_codes.shape[0]
    bin_levels = jnp.arange(BINS, dtype=jnp.int32)

    def add_block(step_index, running):
        start_row = step_index * block_rows
        code_block = lax.dynamic_slice_in_dim(bin_codes, start_row, block_rows, 1)
        grad_block = lax.dynamic_slice_in_dim(grad_rows, start_row, block_rows, 0)
        hess_block = lax.dynamic_slice_in_dim(hess_rows, start_row, block_rows, 0)
        one_hot = (code_block[:, None, :] == bin_levels[None, :, None]).astype(jnp.bfloat16)
        one_hot = one_hot.reshape(feat_count * BINS, block_rows)
        return (
            running[0] + jnp.dot(one_hot, grad_block, preferred_element_type=jnp.float32),
            running[1] + jnp.dot(one_hot, hess_block, preferred_element_type=jnp.float32),
        )

    initial = (
        jnp.zeros((feat_count * BINS, OUT), jnp.float32),
        jnp.zeros((feat_count * BINS,), jnp.float32),
    )
    return lax.fori_loop(0, grad_rows.shape[0] // block_rows, add_block, initial)


def on_device(gradients, hessians, bin_words, children, split_feature, split_bin):
    row_count = lax.axis_size("rows")
    top_bit = row_count.bit_length() - 1
    row_index = lax.axis_index("rows")
    panel_index = lax.axis_index("feat")
    feat_dev = FEATURES // lax.axis_size("feat")
    row_dev = gradients.shape[0]
    slot_count = 2 * row_dev
    block_rows = min(256, slot_count)
    pad_rows = slot_count - row_dev
    grad_rows = jnp.concatenate([gradients, jnp.zeros((pad_rows, OUT), jnp.bfloat16)], 0)
    hess_rows = jnp.concatenate([hessians, jnp.zeros((pad_rows,), jnp.bfloat16)], 0)
    word_rows = jnp.concatenate(
        [bin_words, jnp.zeros((bin_words.shape[0], pad_rows), jnp.int32)], 1
    )
    child_rows = jnp.concatenate([children, jnp.zeros((children.shape[0], pad_rows), jnp.int32)], 1)
    splits_total = split_feature.shape[0]
    collected = jnp.zeros((splits_total, 2, OUT), jnp.float32)
    gain_list = []
    slot_list = []
    for level_index in range(LEVELS):
        cross_bit = top_bit - 1 - level_index
        half_bit = jnp.bitwise_and(jnp.right_shift(row_index, cross_bit), 1)
        living = hess_rows > 0
        staying = living & (child_rows[level_index] == half_bit)
        leaving = living & (child_rows[level_index] != half_bit)
        sent_hess = jnp.where(leaving, hess_rows, jnp.zeros_like(hess_rows))
        got_grad, got_hess, got_words, got_child = (
            swapped(grad_rows, "rows", cross_bit),
            swapped(sent_hess, "rows", cross_bit),
            swapped(as_sent(word_rows), "rows", cross_bit).astype(word_rows.dtype),
            swapped(as_sent(child_rows), "rows", cross_bit).astype(child_rows.dtype),
        )
        accepted = jnp.concatenate([staying, got_hess > 0])
        source, filled = front_index(accepted, slot_count)
        grad_rows = pick_rows(jnp.concatenate([grad_rows, got_grad], 0), source, filled)
        hess_rows = pick_slots(jnp.concatenate([hess_rows, got_hess], 0), source, filled)
        word_rows = pick_columns(jnp.concatenate([word_rows, got_words], 1), source, filled)
        child_rows = pick_columns(jnp.concatenate([child_rows, got_child], 1), source, filled)
        bin_codes = unpack_codes(word_rows)
        hist_grad, hist_hess = build_hist(bin_codes, grad_rows, hess_rows, block_rows)
        group_size = row_count >> level_index + 1
        node_count = 2 ** (level_index + 1)
        node_here = jnp.right_shift(row_index, top_bit - level_index - 1)
        share_grad = hist_grad.reshape(feat_dev, BINS * OUT)
        share_hess = hist_hess.reshape(feat_dev, BINS)
        for step_bit in reversed(range(top_bit - level_index - 1)):
            half_rows = share_grad.shape[0] // 2
            upper_half = jnp.bitwise_and(jnp.right_shift(row_index, step_bit), 1) == 1
            keep_grad = jnp.where(upper_half, share_grad[half_rows:], share_grad[:half_rows])
            give_grad = jnp.where(upper_half, share_grad[:half_rows], share_grad[half_rows:])
            keep_hess = jnp.where(upper_half, share_hess[half_rows:], share_hess[:half_rows])
            give_hess = jnp.where(upper_half, share_hess[:half_rows], share_hess[half_rows:])
            got_partial, got_curv = swapped((give_grad, give_hess), "rows", step_bit)
            share_grad = keep_grad + got_partial
            share_hess = keep_hess + got_curv
        share_count = share_grad.shape[0]
        cumulative = jnp.cumsum(share_grad.reshape(share_count, BINS, OUT), axis=1)
        hess_cum = jnp.cumsum(share_hess, axis=1)
        split_score, right_sum, hess_right = split_terms(cumulative, hess_cum)
        gain_list.append(split_score)
        position = jnp.bitwise_and(row_index, group_size - 1)
        split_slot = node_count - 2 + node_here
        feature_id = split_feature[split_slot]
        bin_id = split_bin[split_slot]
        inner_feature = feature_id % feat_dev
        is_owner = (feature_id // feat_dev == panel_index) & (
            inner_feature // share_count == position
        )
        chosen = (
            (jnp.arange(share_count)[:, None] == inner_feature % share_count)
            & (jnp.arange(BINS)[None, :] == bin_id)
            & is_owner
        )
        left_grad = jnp.sum(jnp.where(chosen[..., None], cumulative, 0.0), axis=(0, 1))
        left_hess = jnp.sum(jnp.where(chosen, hess_cum, 0.0))
        right_grad = jnp.sum(jnp.where(chosen[..., None], right_sum, 0.0), axis=(0, 1))
        right_hess = jnp.sum(jnp.where(chosen, hess_right, 0.0))
        child_pair = jnp.stack(
            [
                -left_grad / jnp.sqrt(left_hess + penalty),
                -right_grad / jnp.sqrt(right_hess + penalty),
            ],
            0,
        )
        slot_match = jnp.arange(splits_total) == split_slot
        collected = collected + jnp.where(slot_match[:, None, None], child_pair[None], 0.0)
        slot_list.append(split_slot)
    totals = lax.psum(collected, ("rows", "feat"))
    child_scores = jnp.stack([totals[slot_index] for slot_index in slot_list], 0)[:, None]
    return (gain_list[0], gain_list[1], gain_list[2], child_scores)


def solution(mesh):
    placed = (P("rows", None), P("rows"), P("feat", "rows"), P(None, "rows"), P(), P())
    return jax.shard_map(
        on_device,
        mesh=mesh,
        in_specs=placed,
        out_specs=(
            P("rows", "feat"),
            P("rows", "feat"),
            P("rows", "feat"),
            P(None, "rows", None, None),
        ),
        check_vma=False,
    )
```

profile of v0, /device:TPU:1, one launch (start us, length us, event | category | flops | bytes accessed | tf_op | source)
XLA Modules:
  0.0 707.1 jit_solution(15301522432196689266)
XLA Ops:
  22.0 74.8 %while.98 = (s32[]{:T(128)}, u32[1024]{0:T(1024)S(1)}, u32[1024]{0:T(1024)S(1)}, s32[2048]{0:T(1024)S(1)}, s32[]{:T(128)}, /*index=5*/s32[]{:T(128)}, s32[]{}) while((s32[]{:T(128)}, u32[1024]{0:T(1024)S(1)}, u32[1024]{0:T(1024)S(1)}, s32[2048]{0:T(1024)S(1)}, s32[]{:T(128)}, /*index=5*/s32[]{:T(128)}, s32[]{}) %tuple.223), condition=%wide.region_3.4_spmd.clone, body=%wide.region_2.3_spmd.clone.sunk | while | flops 20484 | bytes 63589 | solution.py:49
  22.0 6.2 gather_fusion
  28.3 6.2 gather_fusion
  34.5 6.2 gather_fusion
  40.7 6.2 gather_fusion
  97.5 6.8 gather_fusion.5
  112.2 74.8 %while.100 = (s32[]{:T(128)}, u32[1024]{0:T(1024)S(1)}, u32[1024]{0:T(1024)S(1)}, s32[2048]{0:T(1024)S(1)}, s32[]{:T(128)}, /*index=5*/s32[]{:T(128)}, s32[]{}) while((s32[]{:T(128)}, u32[1024]{0:T(1024)S(1)}, u32[1024]{0:T(1024)S(1)}, s32[2048]{0:T(1024)S(1)}, s32[]{:T(128)}, /*index=5*/s32[]{:T(128)}, s32[]{}) %tuple.226), condition=%wide.region_14.19_spmd.clone, body=%wide.region_13.18_spmd.clone.sunk | while | flops 20484 | bytes 63589 | solution.py:49
  188.3 6.8 gather_fusion.9
  199.6 7.0 collective-permute-start.26
  210.8 74.8 %while.102 = (s32[]{:T(128)}, u32[1024]{0:T(1024)S(1)}, u32[1024]{0:T(1024)S(1)}, s32[2048]{0:T(1024)S(1)}, s32[]{:T(128)}, /*index=5*/s32[]{:T(128)}, s32[]{}) while((s32[]{:T(128)}, u32[1024]{0:T(1024)S(1)}, u32[1024]{0:T(1024)S(1)}, s32[2048]{0:T(1024)S(1)}, s32[]{:T(128)}, /*index=5*/s32[]{:T(128)}, s32[]{}) %tuple.229), condition=%wide.region_25.30_spmd.clone, body=%wide.region_24.29_spmd.clone.sunk | while | flops 20484 | bytes 63589 | solution.py:49
  286.2 6.8 gather_fusion.13
  325.9 10.0 %collective-permute-done.27 = s32[32,1024]{0,1:T(8,128)} collective-permute-done((s32[32,1024]{0,1:T(8,128)S(1)}, s32[32,1024]{0,1:T(8,128)}, u32[]{:S(2)}, u32[]{:S(2)}) %collective-permute-start.27) | collective-permute-done | bytes 131104 | tf_op jit(solution)/shard_map/ppermute | solution.py:24
  347.7 14.4 %while.99 = (s32[]{:T(128)}, f32[4096,128]{1,0:T(8,128)S(1)}, f32[4096]{0:T(1024)S(1)}, s32[64,1024]{1,0:T(8,128)}, bf16[1024,128]{1,0:T(8,128)(2,1)S(1)}, /*ind...) while((s32[]{:T(128)}, f32[4096,128]{1,0:T(8,128)S(1)}, ...), condition=%wide.region_5.9_spmd.clone, body=%wide.region_4.8_spmd.clone.sunk | while | flops 272637952 | bytes 7735978 | solution.py:89
  371.3 8.6 %collective-permute-start.10 = (f32[8,64]{1,0:T(8,128)S(1)}, f32[8,64]{1,0:T(8,128)S(1)}, u32[]{:S(2)}, u32[]{:S(2)}) collective-permute-start(f32[8,64]{1,0:T(8,128)S(1)} %slice_select_fusion.26), channel_id=1, source_target_pairs={{0,16},{16,0},{4,20},{20,4},{8,24},{24,8},{12,28},{28,12},{32,48},... | collective-permute-start | bytes 6152 | tf_op jit(solution)/shard_map/ppermute | solution.py:24
  395.3 22.7 %while.101 = (s32[]{:T(128)}, f32[4096,128]{1,0:T(8,128)}, f32[4096]{0:T(1024)S(1)}, s32[64,1024]{1,0:T(8,128)}, bf16[1024,128]{1,0:T(8,128)(2,1)S(1)}, /*index=...) while((s32[]{:T(128)}, f32[4096,128]{1,0:T(8,128)}, ...), condition=%wide.region_16.21_spmd.clone, body=%wide.region_15.20_spmd.clone.sunk | while | flops 272637952 | bytes 7735978 | solution.py:89
  420.2 6.4 collective-permute-start.12
  448.5 17.1 %while.103 = (s32[]{:T(128)}, f32[4096,128]{1,0:T(8,128)S(1)}, f32[4096]{0:T(1024)S(1)}, s32[64,1024]{1,0:T(8,128)}, bf16[1024,128]{1,0:T(8,128)(2,1)S(1)}, /*in...) while((s32[]{:T(128)}, f32[4096,128]{1,0:T(8,128)S(1)}, ...), condition=%wide.region_27.32_spmd.clone, body=%wide.region_26.31_spmd.clone.sunk | while | flops 272637952 | bytes 7735978 | solution.py:89
  465.8 7.1 %collective-permute-start.24 = (f32[4,64]{1,0:T(4,128)S(1)}, f32[4,64]{1,0:T(4,128)S(1)}, u32[]{:S(2)}, u32[]{:S(2)}) collective-permute-start(f32[4,64]{1,0:T(4,128)S(1)} %slice_select_fusion.27), channel_id=1, source_target_pairs={{0,4},{4,0},{8,12},{12,8},{16,20},{20,16},{24,28},{28,24},{32,36},... | collective-permute-start | bytes 3080 | tf_op jit(solution)/shard_map/ppermute | solution.py:24
  472.9 18.8 %collective-permute-done.32 = f32[32,64]{1,0:T(8,128)S(1)} collective-permute-done((f32[32,64]{1,0:T(8,128)S(1)}, f32[32,64]{1,0:T(8,128)S(1)}, u32[]{:S(2)}, u32[]{:S(2)}) %collective-permute-start.32) | collective-permute-done | bytes 8224 | tf_op jit(solution)/shard_map/ppermute | solution.py:24
  508.4 73.3 %collective-permute-done.29 = f32[32,8192]{1,0:T(8,128)} collective-permute-done((f32[32,8192]{1,0:T(8,128)}, f32[32,8192]{1,0:T(8,128)}, u32[]{:S(2)}, u32[]{:S(2)}) %collective-permute-start.29) | collective-permute-done | bytes 1048608 | tf_op jit(solution)/shard_map/ppermute | solution.py:24
  585.3 7.6 %collective-permute-done.18 = f32[16,8192]{1,0:T(8,128)S(1)} collective-permute-done((f32[16,8192]{1,0:T(8,128)S(1)}, f32[16,8192]{1,0:T(8,128)S(1)}, u32[]{:S(2)}, u32[]{:S(2)}) %collective-permute-start.18) | collective-permute-done | bytes 524320 | tf_op jit(solution)/shard_map/ppermute | solution.py:24
  592.9 11.2 %collective-permute-done.5 = f32[8,8192]{1,0:T(8,128)S(1)} collective-permute-done((f32[8,8192]{1,0:T(8,128)S(1)}, f32[8,8192]{1,0:T(8,128)S(1)}, u32[]{:S(2)}, u32[]{:S(2)}) %collective-permute-start.5) | collective-permute-done | bytes 262176 | tf_op jit(solution)/shard_map/ppermute | solution.py:24
  606.1 6.3 collective-permute-done.6
  629.2 76.1 %psum.7 = f32[14,2,128]{2,1,0:T(2,128)S(1)} all-reduce(f32[14,2,128]{2,1,0:T(2,128)S(1)} %select_add_fusion.9), channel_id=1, replica_groups=mesh['rows'=64,'feat'=4] {'rows','feat'}, use_global_device_ids=true, to_apply=%region_45.50 | all-reduce | flops 3584 | bytes 28672 | tf_op jit(solution)/shard_map/psum | solution.py:180
  (596 shorter events, 414.0 us)
Async XLA Ops:
  2.1 18.7 %collective-permute-start = (bf16[1024]{0:T(1024)(128)(2,1)S(1)}, bf16[1024]{0:T(1024)(128)(2,1)S(1)}, u32[]{:S(2)}, u32[]{:S(2)}) collective-permute-start(bf16[1024]{0:T(1024)(128)(2,1)S(1)} %and_select_fusion.2), channel_id=1, source_target_pairs={{0,128},{128,0},{4,132},{132,4},{8,136},{136,8},{12,140},{140,12},... | collective-permute-start | bytes 6152 | tf_op jit(solution)/shard_map/ppermute | solution.py:24
  6.6 97.8 %collective-permute-start.13 = (s32[3,1024]{1,0:T(4,128)S(1)}, s32[3,1024]{1,0:T(4,128)S(1)}, u32[]{:S(2)}, u32[]{:S(2)}) collective-permute-start(s32[3,1024]{1,0:T(4,128)S(1)} %concatenate.74), channel_id=1, source_target_pairs={{0,128},{128,0},{4,132},{132,4},{8,136},{136,8},{12,140},{140,12},... | collective-permute-start | bytes 36872 | tf_op jit(solution)/shard_map/ppermute | solution.py:24
  7.4 285.6 %collective-permute-start.1 = (s32[32,1024]{1,0:T(8,128)S(1)}, s32[32,1024]{1,0:T(8,128)S(1)}, u32[]{:S(2)}, u32[]{:S(2)}) collective-permute-start(s32[32,1024]{1,0:T(8,128)S(1)} %concatenate.78), channel_id=1, source_target_pairs={{0,128},{128,0},{4,132},{132,4},{8,136},{136,8},{12,140},{140,12},... | collective-permute-start | bytes 393224 | tf_op jit(solution)/shard_map/ppermute | solution.py:24
  12.1 306.9 %collective-permute-start.2 = (bf16[1024,128]{1,0:T(8,128)(2,1)}, bf16[1024,128]{1,0:T(8,128)(2,1)}, u32[]{:S(2)}, u32[]{:S(2)}) collective-permute-start(bf16[1024,128]{1,0:T(8,128)(2,1)} %concatenate.80), channel_id=1, source_target_pairs={{0,128},{128,0},{4,132},{132,4},{8,136},{136,8},{12,140},{140,12},... | collective-permute-start | bytes 786440 | tf_op jit(solution)/shard_map/ppermute | solution.py:24
  111.1 84.0 %collective-permute-start.25 = (s32[3,1024]{0,1:T(8,128)S(1)}, s32[3,1024]{0,1:T(8,128)S(1)}, u32[]{:S(2)}, u32[]{:S(2)}) collective-permute-start(s32[3,1024]{0,1:T(8,128)S(1)} %bitcast_select_fusion.2), channel_id=1, source_target_pairs={{0,64},{64,0},{4,68},{68,4},{8,72},{72,8},{12,76},{76,12},{16,80},... | collective-permute-start | bytes 36872 | tf_op jit(solution)/shard_map/ppermute | solution.py:24
  199.6 10.6 %collective-permute-start.26 = (bf16[1024]{0:T(1024)(128)(2,1)S(1)}, bf16[1024]{0:T(1024)(128)(2,1)S(1)}, u32[]{:S(2)}, u32[]{:S(2)}) collective-permute-start(bf16[1024]{0:T(1024)(128)(2,1)S(1)} %and_select_fusion), channel_id=1, source_target_pairs={{0,32},{32,0},{4,36},{36,4},{8,40},{40,8},{12,44},{44,12},{16,48},... | collective-permute-start | bytes 6152 | tf_op jit(solution)/shard_map/ppermute | solution.py:24
  298.8 10.4 %collective-permute-start.15 = (s32[32,1024]{0,1:T(8,128)S(1)}, s32[32,1024]{0,1:T(8,128)}, u32[]{:S(2)}, u32[]{:S(2)}) collective-permute-start(s32[32,1024]{0,1:T(8,128)S(1)} %bitcast_select_fusion.3), channel_id=1, source_target_pairs={{0,64},{64,0},{4,68},{68,4},{8,72},{72,8},{12,76},{76,12},{16,80},... | collective-permute-start | bytes 393224 | tf_op jit(solution)/shard_map/ppermute | solution.py:24
  315.7 20.2 %collective-permute-start.27 = (s32[32,1024]{0,1:T(8,128)S(1)}, s32[32,1024]{0,1:T(8,128)}, u32[]{:S(2)}, u32[]{:S(2)}) collective-permute-start(s32[32,1024]{0,1:T(8,128)S(1)} %bitcast_select_fusion.1), channel_id=1, source_target_pairs={{0,32},{32,0},{4,36},{36,4},{8,40},{40,8},{12,44},{44,12},{16,48},... | collective-permute-start | bytes 393224 | tf_op jit(solution)/shard_map/ppermute | solution.py:24
  371.3 9.9 %collective-permute-start.10 = (f32[8,64]{1,0:T(8,128)S(1)}, f32[8,64]{1,0:T(8,128)S(1)}, u32[]{:S(2)}, u32[]{:S(2)}) collective-permute-start(f32[8,64]{1,0:T(8,128)S(1)} %slice_select_fusion.26), channel_id=1, source_target_pairs={{0,16},{16,0},{4,20},{20,4},{8,24},{24,8},{12,28},{28,12},{32,48},... | collective-permute-start | bytes 6152 | tf_op jit(solution)/shard_map/ppermute | solution.py:24
  379.9 10.8 %collective-permute-start.16 = (bf16[1024,128]{1,0:T(8,128)(2,1)S(1)}, bf16[1024,128]{1,0:T(8,128)(2,1)}, u32[]{:S(2)}, u32[]{:S(2)}) collective-permute-start(bf16[1024,128]{1,0:T(8,128)(2,1)S(1)} %get-tuple-element.1187), channel_id=1, source_target_pairs={{0,64},{64,0},{4,68},{68,4},{8,72},{72,8},{12,76},{76,12},{16,80},... | collective-permute-start | bytes 786440 | tf_op jit(solution)/shard_map/ppermute | solution.py:24
  381.2 9.5 %collective-permute-start.11 = (f32[4,64]{1,0:T(4,128)S(1)}, f32[4,64]{1,0:T(4,128)S(1)}, u32[]{:S(2)}, u32[]{:S(2)}) collective-permute-start(f32[4,64]{1,0:T(4,128)S(1)} %slice_select_fusion.28), channel_id=1, source_target_pairs={{0,8},{8,0},{4,12},{12,4},{16,24},{24,16},{20,28},{28,20},{32,40},... | collective-permute-start | bytes 3080 | tf_op jit(solution)/shard_map/ppermute | solution.py:24
  388.2 112.1 %collective-permute-start.3 = (f32[32,8192]{1,0:T(8,128)}, f32[32,8192]{1,0:T(8,128)}, u32[]{:S(2)}, u32[]{:S(2)}) collective-permute-start(f32[32,8192]{1,0:T(8,128)} %select_n.551), channel_id=1, source_target_pairs={{0,64},{64,0},{4,68},{68,4},{8,72},{72,8},{12,76},{76,12},{16,80},... | collective-permute-start | bytes 3145736 | tf_op jit(solution)/shard_map/ppermute | solution.py:24
  418.1 8.6 %collective-permute-start.21 = (f32[32,64]{1,0:T(8,128)S(1)}, f32[32,64]{1,0:T(8,128)S(1)}, u32[]{:S(2)}, u32[]{:S(2)}) collective-permute-start(f32[32,64]{1,0:T(8,128)S(1)} %select_n.603), channel_id=1, source_target_pairs={{0,32},{32,0},{4,36},{36,4},{8,40},{40,8},{12,44},{44,12},{16,48},... | collective-permute-start | bytes 24584 | tf_op jit(solution)/shard_map/ppermute | solution.py:24
  427.7 16.2 %collective-permute-start.28 = (bf16[1024,128]{1,0:T(8,128)(2,1)S(1)}, bf16[1024,128]{1,0:T(8,128)(2,1)}, u32[]{:S(2)}, u32[]{:S(2)}) collective-permute-start(bf16[1024,128]{1,0:T(8,128)(2,1)S(1)} %get-tuple-element.1189), channel_id=1, source_target_pairs={{0,32},{32,0},{4,36},{36,4},{8,40},{40,8},{12,44},{44,12},{16,48},... | collective-permute-start | bytes 786440 | tf_op jit(solution)/shard_map/ppermute | solution.py:24
  431.2 12.7 %collective-permute-start.23 = (f32[8,64]{1,0:T(8,128)S(1)}, f32[8,64]{1,0:T(8,128)S(1)}, u32[]{:S(2)}, u32[]{:S(2)}) collective-permute-start(f32[8,64]{1,0:T(8,128)S(1)} %slice_select_fusion.25), channel_id=1, source_target_pairs={{0,8},{8,0},{4,12},{12,4},{16,24},{24,16},{20,28},{28,20},{32,40},... | collective-permute-start | bytes 6152 | tf_op jit(solution)/shard_map/ppermute | solution.py:24
  437.7 67.3 %collective-permute-start.17 = (f32[32,8192]{1,0:T(8,128)}, f32[32,8192]{1,0:T(8,128)}, u32[]{:S(2)}, u32[]{:S(2)}) collective-permute-start(f32[32,8192]{1,0:T(8,128)} %select_n.589), channel_id=1, source_target_pairs={{0,32},{32,0},{4,36},{36,4},{8,40},{40,8},{12,44},{44,12},{16,48},... | collective-permute-start | bytes 3145736 | tf_op jit(solution)/shard_map/ppermute | solution.py:24
  465.7 26.0 %collective-permute-start.32 = (f32[32,64]{1,0:T(8,128)S(1)}, f32[32,64]{1,0:T(8,128)S(1)}, u32[]{:S(2)}, u32[]{:S(2)}) collective-permute-start(f32[32,64]{1,0:T(8,128)S(1)} %select_n.632), channel_id=1, source_target_pairs={{0,16},{16,0},{4,20},{20,4},{8,24},{24,8},{12,28},{28,12},{32,48},... | collective-permute-start | bytes 24584 | tf_op jit(solution)/shard_map/ppermute | solution.py:24
  465.8 26.0 %collective-permute-start.24 = (f32[4,64]{1,0:T(4,128)S(1)}, f32[4,64]{1,0:T(4,128)S(1)}, u32[]{:S(2)}, u32[]{:S(2)}) collective-permute-start(f32[4,64]{1,0:T(4,128)S(1)} %slice_select_fusion.27), channel_id=1, source_target_pairs={{0,4},{4,0},{8,12},{12,8},{16,20},{20,16},{24,28},{28,24},{32,36},... | collective-permute-start | bytes 3080 | tf_op jit(solution)/shard_map/ppermute | solution.py:24
  499.5 82.2 %collective-permute-start.29 = (f32[32,8192]{1,0:T(8,128)}, f32[32,8192]{1,0:T(8,128)}, u32[]{:S(2)}, u32[]{:S(2)}) collective-permute-start(f32[32,8192]{1,0:T(8,128)} %select_n.621), channel_id=1, source_target_pairs={{0,16},{16,0},{4,20},{20,4},{8,24},{24,8},{12,28},{28,12},{32,48},... | collective-permute-start | bytes 3145736 | tf_op jit(solution)/shard_map/ppermute | solution.py:24
  501.8 81.4 %collective-permute-start.4 = (f32[16,8192]{1,0:T(8,128)S(1)}, f32[16,8192]{1,0:T(8,128)S(1)}, u32[]{:S(2)}, u32[]{:S(2)}) collective-permute-start(f32[16,8192]{1,0:T(8,128)S(1)} %slice_select_fusion.9), channel_id=1, source_target_pairs={{0,32},{32,0},{4,36},{36,4},{8,40},{40,8},{12,44},{44,12},{16,48},... | collective-permute-start | bytes 1572872 | tf_op jit(solution)/shard_map/ppermute | solution.py:24
  506.4 86.4 %collective-permute-start.18 = (f32[16,8192]{1,0:T(8,128)S(1)}, f32[16,8192]{1,0:T(8,128)S(1)}, u32[]{:S(2)}, u32[]{:S(2)}) collective-permute-start(f32[16,8192]{1,0:T(8,128)S(1)} %slice_select_fusion.8), channel_id=1, source_target_pairs={{0,16},{16,0},{4,20},{20,4},{8,24},{24,8},{12,28},{28,12},{32,48},... | collective-permute-start | bytes 1572872 | tf_op jit(solution)/shard_map/ppermute | solution.py:24
  583.0 35.7 %collective-permute-start.30 = (f32[16,8192]{1,0:T(8,128)S(1)}, f32[16,8192]{1,0:T(8,128)S(1)}, u32[]{:S(2)}, u32[]{:S(2)}) collective-permute-start(f32[16,8192]{1,0:T(8,128)S(1)} %slice_select_fusion.7), channel_id=1, source_target_pairs={{0,8},{8,0},{4,12},{12,4},{16,24},{24,16},{20,28},{28,20},{32,40},... | collective-permute-start | bytes 1572872 | tf_op jit(solution)/shard_map/ppermute | solution.py:24
  583.3 20.8 %collective-permute-start.5 = (f32[8,8192]{1,0:T(8,128)S(1)}, f32[8,8192]{1,0:T(8,128)S(1)}, u32[]{:S(2)}, u32[]{:S(2)}) collective-permute-start(f32[8,8192]{1,0:T(8,128)S(1)} %slice_select_fusion.12), channel_id=1, source_target_pairs={{0,16},{16,0},{4,20},{20,4},{8,24},{24,8},{12,28},{28,12},{32,48},... | collective-permute-start | bytes 786440 | tf_op jit(solution)/shard_map/ppermute | solution.py:24
  604.6 13.4 %collective-permute-start.19 = (f32[8,8192]{1,0:T(8,128)S(1)}, f32[8,8192]{1,0:T(8,128)S(1)}, u32[]{:S(2)}, u32[]{:S(2)}) collective-permute-start(f32[8,8192]{1,0:T(8,128)S(1)} %slice_select_fusion.11), channel_id=1, source_target_pairs={{0,8},{8,0},{4,12},{12,4},{16,24},{24,16},{20,28},{28,20},{32,40},... | collective-permute-start | bytes 786440 | tf_op jit(solution)/shard_map/ppermute | solution.py:24
  (32 other events, 303.9 us)
where the time goes:
time: 718 us; the launch traced here: 707 us
  local copies, waits for them, and re-layouts  310 us (43%)
  waiting for transfers between devices  148 us (21%)
  blocking collectives  76.1 us (11%)
  starting transfers between devices  69.2 us (10%)
  other arithmetic  58 us (8%)
  matrix products  30.3 us (4%)
  between operations  13.7 us (2%)
    gather x36, local copies, waits for them, and re-layouts, front_index(): source = jnp.searchsorted(running, wanted, side='left')  222 us
    ppermute x35, waiting for transfers between devices, swapped(): return lax.ppermute(block, axis, route)  148 us
    psum x1, blocking collectives, on_device(): totals = lax.psum(collected, ('rows', 'feat'))  76.1 us
    ppermute x35, starting transfers between devices, swapped(): return lax.ppermute(block, axis, route)  69.2 us
    dot_general x12, matrix products, add_block(): jnp.dot(one_hot, grad_block, preferred_element_type=jnp.float32)  22.6 us
    gather x3, local copies, waits for them, and re-layouts, pick_slots(): taken = jnp.take(values, source, axis=0)  20.4 us
    gather x5, local copies, waits for them, and re-layouts, pick_columns(): taken = jnp.take(values, source, axis=1)  19 us
  transfers between devices with their start and end apart: 35, of which 14 were waited for; matrix products, arithmetic and copies ran while one was open for 52% of the time, Pallas kernels for 0%

commit v1 on v0

--- a/solution.py
+++ b/solution.py
@@ -8,6 +8,12 @@
 OUT = 128
 LEVELS = 3
 penalty = 1.0
+
+
+def gather_and_add(x, mesh_axis):
+    parts = lax.all_gather(x, mesh_axis, axis=0, tiled=False)
+    total = parts.sum(axis=0)
+    return total
 
 
 def as_sent(array):
@@ -177,7 +183,7 @@
         slot_match = jnp.arange(splits_total) == split_slot
         collected = collected + jnp.where(slot_match[:, None, None], child_pair[None], 0.0)
         slot_list.append(split_slot)
-    totals = lax.psum(collected, ("rows", "feat"))
+    totals = gather_and_add(collected, ("rows", "feat"))
     child_scores = jnp.stack([totals[slot_index] for slot_index in slot_list], 0)[:, None]
     return (gain_list[0], gain_list[1], gain_list[2], child_scores)
 

time: 718 us -> 771 us (1.074)
  waiting for transfers between devices: 148 us -> 260 us
  blocking collectives: 76.1 us -> 0 us
  between operations: 13.7 us -> 27.2 us
    all_gather x0 -> x1, waiting for transfers between devices: none -> 112 us  [gather_and_add(): parts = lax.all_gather(x, mesh_axis, axis=0, tiled=False)]
    psum x1 -> x0, blocking collectives: 76.1 us -> none  [on_device(): totals = lax.psum(collected, ('rows', 'feat'))]
  transfers between devices with their start and end apart: 35 -> 36, of which waited for: 14 -> 15; matrix products, arithmetic and copies ran while one was open for 52% -> 48% of each run, Pallas kernels for 0% -> 0%
where the time goes in v1:
time: 771 us; the launch traced here: 761 us
  local copies, waits for them, and re-layouts  310 us (40%)
  waiting for transfers between devices  260 us (34%)
  starting transfers between devices  69.2 us (9%)
  other arithmetic  61.7 us (8%)
  matrix products  30.3 us (4%)
  between operations  27.2 us (4%)
    gather x36, local copies, waits for them, and re-layouts, front_index(): source = jnp.searchsorted(running, wanted, side='left')  222 us
    ppermute x35, waiting for transfers between devices, swapped(): return lax.ppermute(block, axis, route)  148 us
    all_gather x1, waiting for transfers between devices, gather_and_add(): parts = lax.all_gather(x, mesh_axis, axis=0, tiled=False)  112 us
    ppermute x35, starting transfers between devices, swapped(): return lax.ppermute(block, axis, route)  69.2 us
    dot_general x12, matrix products, add_block(): jnp.dot(one_hot, grad_block, preferred_element_type=jnp.float32)  22.6 us
    gather x3, local copies, waits for them, and re-layouts, pick_slots(): taken = jnp.take(values, source, axis=0)  20.4 us
    gather x5, local copies, waits for them, and re-layouts, pick_columns(): taken = jnp.take(values, source, axis=1)  19 us
  transfers between devices with their start and end apart: 36, of which 15 were waited for; matrix products, arithmetic and copies ran while one was open for 48% of the time, Pallas kernels for 0%

profile of v1, /device:TPU:1, one launch (start us, length us, event | category | flops | bytes accessed | tf_op | source)
XLA Modules:
  0.0 760.7 jit_solution(2612169343144147408)
XLA Ops:
  28.6 74.8 %while.98 = (s32[]{:T(128)}, u32[1024]{0:T(1024)S(1)}, u32[1024]{0:T(1024)S(1)}, s32[2048]{0:T(1024)S(1)}, s32[]{:T(128)}, /*index=5*/s32[]{:T(128)}, s32[]{}) while((s32[]{:T(128)}, u32[1024]{0:T(1024)S(1)}, u32[1024]{0:T(1024)S(1)}, s32[2048]{0:T(1024)S(1)}, s32[]{:T(128)}, /*index=5*/s32[]{:T(128)}, s32[]{}) %tuple.223), condition=%wide.region_3.4_spmd.clone, body=%wide.region_2.3_spmd.clone.sunk | while | flops 20484 | bytes 63589 | solution.py:55
  28.6 6.2 gather_fusion
  34.8 6.2 gather_fusion
  41.1 6.2 gather_fusion
  47.3 6.2 gather_fusion
  104.1 6.8 gather_fusion.5
  118.8 74.8 %while.100 = (s32[]{:T(128)}, u32[1024]{0:T(1024)S(1)}, u32[1024]{0:T(1024)S(1)}, s32[2048]{0:T(1024)S(1)}, s32[]{:T(128)}, /*index=5*/s32[]{:T(128)}, s32[]{}) while((s32[]{:T(128)}, u32[1024]{0:T(1024)S(1)}, u32[1024]{0:T(1024)S(1)}, s32[2048]{0:T(1024)S(1)}, s32[]{:T(128)}, /*index=5*/s32[]{:T(128)}, s32[]{}) %tuple.226), condition=%wide.region_14.19_spmd.clone, body=%wide.region_13.18_spmd.clone.sunk | while | flops 20484 | bytes 63589 | solution.py:55
  194.9 6.8 gather_fusion.9
  206.2 7.0 collective-permute-start.26
  217.4 74.8 %while.102 = (s32[]{:T(128)}, u32[1024]{0:T(1024)S(1)}, u32[1024]{0:T(1024)S(1)}, s32[2048]{0:T(1024)S(1)}, s32[]{:T(128)}, /*index=5*/s32[]{:T(128)}, s32[]{}) while((s32[]{:T(128)}, u32[1024]{0:T(1024)S(1)}, u32[1024]{0:T(1024)S(1)}, s32[2048]{0:T(1024)S(1)}, s32[]{:T(128)}, /*index=5*/s32[]{:T(128)}, s32[]{}) %tuple.229), condition=%wide.region_25.30_spmd.clone, body=%wide.region_24.29_spmd.clone.sunk | while | flops 20484 | bytes 63589 | solution.py:55
  292.8 6.8 gather_fusion.13
  332.5 10.0 %collective-permute-done.27 = s32[32,1024]{0,1:T(8,128)} collective-permute-done((s32[32,1024]{0,1:T(8,128)S(1)}, s32[32,1024]{0,1:T(8,128)}, u32[]{:S(2)}, u32[]{:S(2)}) %collective-permute-start.27) | collective-permute-done | bytes 131104 | tf_op jit(solution)/shard_map/ppermute | solution.py:30
  354.3 14.4 %while.99 = (s32[]{:T(128)}, f32[4096,128]{1,0:T(8,128)S(1)}, f32[4096]{0:T(1024)S(1)}, s32[64,1024]{1,0:T(8,128)}, bf16[1024,128]{1,0:T(8,128)(2,1)S(1)}, /*ind...) while((s32[]{:T(128)}, f32[4096,128]{1,0:T(8,128)S(1)}, ...), condition=%wide.region_5.9_spmd.clone, body=%wide.region_4.8_spmd.clone.sunk | while | flops 272637952 | bytes 7735978 | solution.py:95
  377.9 8.6 %collective-permute-start.10 = (f32[8,64]{1,0:T(8,128)S(1)}, f32[8,64]{1,0:T(8,128)S(1)}, u32[]{:S(2)}, u32[]{:S(2)}) collective-permute-start(f32[8,64]{1,0:T(8,128)S(1)} %slice_select_fusion.26), channel_id=1, source_target_pairs={{0,16},{16,0},{4,20},{20,4},{8,24},{24,8},{12,28},{28,12},{32,48},... | collective-permute-start | bytes 6152 | tf_op jit(solution)/shard_map/ppermute | solution.py:30
  401.8 22.7 %while.101 = (s32[]{:T(128)}, f32[4096,128]{1,0:T(8,128)}, f32[4096]{0:T(1024)S(1)}, s32[64,1024]{1,0:T(8,128)}, bf16[1024,128]{1,0:T(8,128)(2,1)S(1)}, /*index=...) while((s32[]{:T(128)}, f32[4096,128]{1,0:T(8,128)}, ...), condition=%wide.region_16.21_spmd.clone, body=%wide.region_15.20_spmd.clone.sunk | while | flops 272637952 | bytes 7735978 | solution.py:95
  426.8 6.4 collective-permute-start.12
  455.1 17.1 %while.103 = (s32[]{:T(128)}, f32[4096,128]{1,0:T(8,128)S(1)}, f32[4096]{0:T(1024)S(1)}, s32[64,1024]{1,0:T(8,128)}, bf16[1024,128]{1,0:T(8,128)(2,1)S(1)}, /*in...) while((s32[]{:T(128)}, f32[4096,128]{1,0:T(8,128)S(1)}, ...), condition=%wide.region_27.32_spmd.clone, body=%wide.region_26.31_spmd.clone.sunk | while | flops 272637952 | bytes 7735978 | solution.py:95
  472.4 7.1 collective-permute-start.24
  479.5 18.7 %collective-permute-done.32 = f32[32,64]{1,0:T(8,128)S(1)} collective-permute-done((f32[32,64]{1,0:T(8,128)S(1)}, f32[32,64]{1,0:T(8,128)S(1)}, u32[]{:S(2)}, u32[]{:S(2)}) %collective-permute-start.32) | collective-permute-done | bytes 8224 | tf_op jit(solution)/shard_map/ppermute | solution.py:30
  514.9 73.3 %collective-permute-done.29 = f32[32,8192]{1,0:T(8,128)} collective-permute-done((f32[32,8192]{1,0:T(8,128)}, f32[32,8192]{1,0:T(8,128)}, u32[]{:S(2)}, u32[]{:S(2)}) %collective-permute-start.29) | collective-permute-done | bytes 1048608 | tf_op jit(solution)/shard_map/ppermute | solution.py:30
  591.8 7.6 collective-permute-done.18
  599.5 11.2 %collective-permute-done.5 = f32[8,8192]{1,0:T(8,128)S(1)} collective-permute-done((f32[8,8192]{1,0:T(8,128)S(1)}, f32[8,8192]{1,0:T(8,128)S(1)}, u32[]{:S(2)}, u32[]{:S(2)}) %collective-permute-start.5) | collective-permute-done | bytes 262176 | tf_op jit(solution)/shard_map/ppermute | solution.py:30
  612.7 6.3 collective-permute-done.6
  637.2 112.5 %all-gather.2.cloned.1.call-done = f32[256,14,2,128]{3,2,1,0:T(2,128)} async-done(((f32[1,14,2,128]{3,2,1,0:T(2,128)}), f32[256,14,2,128]{3,2,1,0:T(2,128)}) %all-gather.2.cloned.1.call-update) | async-done | bytes 3670032 | tf_op jit(solution)/shard_map/all_gather | solution.py:14
  (599 shorter events, 417.7 us)
Async XLA Ops:
  7.2 742.6 %all-gather.2.cloned.1.call-start = ((), (), s32[]{:S(2)}) async-start(), calls=%async_computation | async-start | bytes 3684352 | tf_op jit(solution)/shard_map/all_gather | solution.py:14
  8.7 18.7 %collective-permute-start = (bf16[1024]{0:T(1024)(128)(2,1)S(1)}, bf16[1024]{0:T(1024)(128)(2,1)S(1)}, u32[]{:S(2)}, u32[]{:S(2)}) collective-permute-start(bf16[1024]{0:T(1024)(128)(2,1)S(1)} %and_select_fusion.2), channel_id=1, source_target_pairs={{0,128},{128,0},{4,132},{132,4},{8,136},{136,8},{12,140},{140,12},... | collective-permute-start | bytes 6152 | tf_op jit(solution)/shard_map/ppermute | solution.py:30
  13.1 97.8 %collective-permute-start.13 = (s32[3,1024]{1,0:T(4,128)S(1)}, s32[3,1024]{1,0:T(4,128)S(1)}, u32[]{:S(2)}, u32[]{:S(2)}) collective-permute-start(s32[3,1024]{1,0:T(4,128)S(1)} %concatenate.74), channel_id=1, source_target_pairs={{0,128},{128,0},{4,132},{132,4},{8,136},{136,8},{12,140},{140,12},... | collective-permute-start | bytes 36872 | tf_op jit(solution)/shard_map/ppermute | solution.py:30
  14.0 285.6 %collective-permute-start.1 = (s32[32,1024]{1,0:T(8,128)S(1)}, s32[32,1024]{1,0:T(8,128)S(1)}, u32[]{:S(2)}, u32[]{:S(2)}) collective-permute-start(s32[32,1024]{1,0:T(8,128)S(1)} %concatenate.78), channel_id=1, source_target_pairs={{0,128},{128,0},{4,132},{132,4},{8,136},{136,8},{12,140},{140,12},... | collective-permute-start | bytes 393224 | tf_op jit(solution)/shard_map/ppermute | solution.py:30
  18.7 306.9 %collective-permute-start.2 = (bf16[1024,128]{1,0:T(8,128)(2,1)}, bf16[1024,128]{1,0:T(8,128)(2,1)}, u32[]{:S(2)}, u32[]{:S(2)}) collective-permute-start(bf16[1024,128]{1,0:T(8,128)(2,1)} %concatenate.80), channel_id=1, source_target_pairs={{0,128},{128,0},{4,132},{132,4},{8,136},{136,8},{12,140},{140,12},... | collective-permute-start | bytes 786440 | tf_op jit(solution)/shard_map/ppermute | solution.py:30
  117.7 84.0 %collective-permute-start.25 = (s32[3,1024]{0,1:T(8,128)S(1)}, s32[3,1024]{0,1:T(8,128)S(1)}, u32[]{:S(2)}, u32[]{:S(2)}) collective-permute-start(s32[3,1024]{0,1:T(8,128)S(1)} %bitcast_select_fusion.2), channel_id=1, source_target_pairs={{0,64},{64,0},{4,68},{68,4},{8,72},{72,8},{12,76},{76,12},{16,80},... | collective-permute-start | bytes 36872 | tf_op jit(solution)/shard_map/ppermute | solution.py:30
  206.2 10.6 %collective-permute-start.26 = (bf16[1024]{0:T(1024)(128)(2,1)S(1)}, bf16[1024]{0:T(1024)(128)(2,1)S(1)}, u32[]{:S(2)}, u32[]{:S(2)}) collective-permute-start(bf16[1024]{0:T(1024)(128)(2,1)S(1)} %and_select_fusion), channel_id=1, source_target_pairs={{0,32},{32,0},{4,36},{36,4},{8,40},{40,8},{12,44},{44,12},{16,48},... | collective-permute-start | bytes 6152 | tf_op jit(solution)/shard_map/ppermute | solution.py:30
  305.4 10.4 %collective-permute-start.15 = (s32[32,1024]{0,1:T(8,128)S(1)}, s32[32,1024]{0,1:T(8,128)}, u32[]{:S(2)}, u32[]{:S(2)}) collective-permute-start(s32[32,1024]{0,1:T(8,128)S(1)} %bitcast_select_fusion.3), channel_id=1, source_target_pairs={{0,64},{64,0},{4,68},{68,4},{8,72},{72,8},{12,76},{76,12},{16,80},... | collective-permute-start | bytes 393224 | tf_op jit(solution)/shard_map/ppermute | solution.py:30
  322.3 20.2 %collective-permute-start.27 = (s32[32,1024]{0,1:T(8,128)S(1)}, s32[32,1024]{0,1:T(8,128)}, u32[]{:S(2)}, u32[]{:S(2)}) collective-permute-start(s32[32,1024]{0,1:T(8,128)S(1)} %bitcast_select_fusion.1), channel_id=1, source_target_pairs={{0,32},{32,0},{4,36},{36,4},{8,40},{40,8},{12,44},{44,12},{16,48},... | collective-permute-start | bytes 393224 | tf_op jit(solution)/shard_map/ppermute | solution.py:30
  377.9 9.9 %collective-permute-start.10 = (f32[8,64]{1,0:T(8,128)S(1)}, f32[8,64]{1,0:T(8,128)S(1)}, u32[]{:S(2)}, u32[]{:S(2)}) collective-permute-start(f32[8,64]{1,0:T(8,128)S(1)} %slice_select_fusion.26), channel_id=1, source_target_pairs={{0,16},{16,0},{4,20},{20,4},{8,24},{24,8},{12,28},{28,12},{32,48},... | collective-permute-start | bytes 6152 | tf_op jit(solution)/shard_map/ppermute | solution.py:30
  386.5 10.8 %collective-permute-start.16 = (bf16[1024,128]{1,0:T(8,128)(2,1)S(1)}, bf16[1024,128]{1,0:T(8,128)(2,1)}, u32[]{:S(2)}, u32[]{:S(2)}) collective-permute-start(bf16[1024,128]{1,0:T(8,128)(2,1)S(1)} %get-tuple-element.1189), channel_id=1, source_target_pairs={{0,64},{64,0},{4,68},{68,4},{8,72},{72,8},{12,76},{76,12},{16,80},... | collective-permute-start | bytes 786440 | tf_op jit(solution)/shard_map/ppermute | solution.py:30
  387.8 9.5 %collective-permute-start.11 = (f32[4,64]{1,0:T(4,128)S(1)}, f32[4,64]{1,0:T(4,128)S(1)}, u32[]{:S(2)}, u32[]{:S(2)}) collective-permute-start(f32[4,64]{1,0:T(4,128)S(1)} %slice_select_fusion.28), channel_id=1, source_target_pairs={{0,8},{8,0},{4,12},{12,4},{16,24},{24,16},{20,28},{28,20},{32,40},... | collective-permute-start | bytes 3080 | tf_op jit(solution)/shard_map/ppermute | solution.py:30
  394.8 112.1 %collective-permute-start.3 = (f32[32,8192]{1,0:T(8,128)}, f32[32,8192]{1,0:T(8,128)}, u32[]{:S(2)}, u32[]{:S(2)}) collective-permute-start(f32[32,8192]{1,0:T(8,128)} %select_n.572), channel_id=1, source_target_pairs={{0,64},{64,0},{4,68},{68,4},{8,72},{72,8},{12,76},{76,12},{16,80},... | collective-permute-start | bytes 3145736 | tf_op jit(solution)/shard_map/ppermute | solution.py:30
  434.3 16.2 %collective-permute-start.28 = (bf16[1024,128]{1,0:T(8,128)(2,1)S(1)}, bf16[1024,128]{1,0:T(8,128)(2,1)}, u32[]{:S(2)}, u32[]{:S(2)}) collective-permute-start(bf16[1024,128]{1,0:T(8,128)(2,1)S(1)} %get-tuple-element.1191), channel_id=1, source_target_pairs={{0,32},{32,0},{4,36},{36,4},{8,40},{40,8},{12,44},{44,12},{16,48},... | collective-permute-start | bytes 786440 | tf_op jit(solution)/shard_map/ppermute | solution.py:30
  437.8 12.7 %collective-permute-start.23 = (f32[8,64]{1,0:T(8,128)S(1)}, f32[8,64]{1,0:T(8,128)S(1)}, u32[]{:S(2)}, u32[]{:S(2)}) collective-permute-start(f32[8,64]{1,0:T(8,128)S(1)} %slice_select_fusion.25), channel_id=1, source_target_pairs={{0,8},{8,0},{4,12},{12,4},{16,24},{24,16},{20,28},{28,20},{32,40},... | collective-permute-start | bytes 6152 | tf_op jit(solution)/shard_map/ppermute | solution.py:30
  444.2 67.3 %collective-permute-start.17 = (f32[32,8192]{1,0:T(8,128)}, f32[32,8192]{1,0:T(8,128)}, u32[]{:S(2)}, u32[]{:S(2)}) collective-permute-start(f32[32,8192]{1,0:T(8,128)} %select_n.610), channel_id=1, source_target_pairs={{0,32},{32,0},{4,36},{36,4},{8,40},{40,8},{12,44},{44,12},{16,48},... | collective-permute-start | bytes 3145736 | tf_op jit(solution)/shard_map/ppermute | solution.py:30
  472.3 26.0 %collective-permute-start.32 = (f32[32,64]{1,0:T(8,128)S(1)}, f32[32,64]{1,0:T(8,128)S(1)}, u32[]{:S(2)}, u32[]{:S(2)}) collective-permute-start(f32[32,64]{1,0:T(8,128)S(1)} %select_n.653), channel_id=1, source_target_pairs={{0,16},{16,0},{4,20},{20,4},{8,24},{24,8},{12,28},{28,12},{32,48},... | collective-permute-start | bytes 24584 | tf_op jit(solution)/shard_map/ppermute | solution.py:30
  472.4 26.0 %collective-permute-start.24 = (f32[4,64]{1,0:T(4,128)S(1)}, f32[4,64]{1,0:T(4,128)S(1)}, u32[]{:S(2)}, u32[]{:S(2)}) collective-permute-start(f32[4,64]{1,0:T(4,128)S(1)} %slice_select_fusion.27), channel_id=1, source_target_pairs={{0,4},{4,0},{8,12},{12,8},{16,20},{20,16},{24,28},{28,24},{32,36},... | collective-permute-start | bytes 3080 | tf_op jit(solution)/shard_map/ppermute | solution.py:30
  506.0 82.2 %collective-permute-start.29 = (f32[32,8192]{1,0:T(8,128)}, f32[32,8192]{1,0:T(8,128)}, u32[]{:S(2)}, u32[]{:S(2)}) collective-permute-start(f32[32,8192]{1,0:T(8,128)} %select_n.642), channel_id=1, source_target_pairs={{0,16},{16,0},{4,20},{20,4},{8,24},{24,8},{12,28},{28,12},{32,48},... | collective-permute-start | bytes 3145736 | tf_op jit(solution)/shard_map/ppermute | solution.py:30
  508.4 81.4 %collective-permute-start.4 = (f32[16,8192]{1,0:T(8,128)S(1)}, f32[16,8192]{1,0:T(8,128)S(1)}, u32[]{:S(2)}, u32[]{:S(2)}) collective-permute-start(f32[16,8192]{1,0:T(8,128)S(1)} %slice_select_fusion.9), channel_id=1, source_target_pairs={{0,32},{32,0},{4,36},{36,4},{8,40},{40,8},{12,44},{44,12},{16,48},... | collective-permute-start | bytes 1572872 | tf_op jit(solution)/shard_map/ppermute | solution.py:30
  513.0 86.4 %collective-permute-start.18 = (f32[16,8192]{1,0:T(8,128)S(1)}, f32[16,8192]{1,0:T(8,128)S(1)}, u32[]{:S(2)}, u32[]{:S(2)}) collective-permute-start(f32[16,8192]{1,0:T(8,128)S(1)} %slice_select_fusion.8), channel_id=1, source_target_pairs={{0,16},{16,0},{4,20},{20,4},{8,24},{24,8},{12,28},{28,12},{32,48},... | collective-permute-start | bytes 1572872 | tf_op jit(solution)/shard_map/ppermute | solution.py:30
  589.6 35.7 %collective-permute-start.30 = (f32[16,8192]{1,0:T(8,128)S(1)}, f32[16,8192]{1,0:T(8,128)S(1)}, u32[]{:S(2)}, u32[]{:S(2)}) collective-permute-start(f32[16,8192]{1,0:T(8,128)S(1)} %slice_select_fusion.7), channel_id=1, source_target_pairs={{0,8},{8,0},{4,12},{12,4},{16,24},{24,16},{20,28},{28,20},{32,40},... | collective-permute-start | bytes 1572872 | tf_op jit(solution)/shard_map/ppermute | solution.py:30
  589.8 20.8 %collective-permute-start.5 = (f32[8,8192]{1,0:T(8,128)S(1)}, f32[8,8192]{1,0:T(8,128)S(1)}, u32[]{:S(2)}, u32[]{:S(2)}) collective-permute-start(f32[8,8192]{1,0:T(8,128)S(1)} %slice_select_fusion.12), channel_id=1, source_target_pairs={{0,16},{16,0},{4,20},{20,4},{8,24},{24,8},{12,28},{28,12},{32,48},... | collective-permute-start | bytes 786440 | tf_op jit(solution)/shard_map/ppermute | solution.py:30
  611.2 13.4 %collective-permute-start.19 = (f32[8,8192]{1,0:T(8,128)S(1)}, f32[8,8192]{1,0:T(8,128)S(1)}, u32[]{:S(2)}, u32[]{:S(2)}) collective-permute-start(f32[8,8192]{1,0:T(8,128)S(1)} %slice_select_fusion.11), channel_id=1, source_target_pairs={{0,8},{8,0},{4,12},{12,4},{16,24},{24,16},{20,28},{28,20},{32,40},... | collective-permute-start | bytes 786440 | tf_op jit(solution)/shard_map/ppermute | solution.py:30
  (33 other events, 302.9 us)
Sparse Core Ops, SparseCore 0:
  635.2 114.4 all-gather.1
